TPU v7x, 512 devices: a whole 4x8x8 slice. The times are simulated.
512 devices in a mesh: dp: 32 (over y, z_lo, core), ctx: 16 (over x, z_hi).
Axes of the slice: x: 4, y: 8, z: 8 (z_hi: 4, z_lo: 2; z = z_hi * 2 + z_lo), core: 2. Of those that a mesh axis runs over, the one named last changes fastest.
Arguments:
- queries: bfloat16 [32, 2048, 2048], P('dp', 'ctx'), may hold values from -21 to 21
- keys: bfloat16 [32, 2048, 512], P('dp', 'ctx'), may hold values from -21 to 21
- values: bfloat16 [32, 2048, 512], P('dp', 'ctx'), may hold values from -6 to 6
- dout: bfloat16 [32, 2048, 2048], P('dp', 'ctx'), may hold values from -6 to 6
- sinks: float32 [16], replicated, may hold values from 0 to 6
Outputs:
- grad_queries: bfloat16 [32, 2048, 2048], P('dp', 'ctx')
- grad_keys: bfloat16 [32, 2048, 512], P('dp', 'ctx')
- grad_values: bfloat16 [32, 2048, 512], P('dp', 'ctx')
- sink_grad: float32 [16], replicated
All inputs are finite; a program needn't handle non-finite values.
Results may differ from a plain program's by a relative error of at most 0.03.
Values may be sent and summed in bfloat16 or wider, within the bound.
A program may use at most 64 MiB of HBM per device.

v0:
```python
import jax
import jax.numpy as jnp
from jax import lax
from jax.sharding import PartitionSpec as P

HEADS = 16
KV_HEADS = 4
HEAD = 128
WINDOW = 128


def shifted(value, axis, steps):
    count = lax.axis_size(axis)
    leading, last = (max(0, -steps), min(count, count - steps))
    return lax.ppermute(value, axis, [(source, source + steps) for source in range(leading, last)])


def as_sent(x):
    return jax.tree.map(lambda a: a.astype(jnp.bfloat16) if a.dtype == jnp.float32 else a, x)


def block_terms(query_rows, key_rows, value_rows, grad_rows, sinks, allowed):
    group_size = HEADS // KV_HEADS
    row_count = query_rows.shape[0]
    key_count = key_rows.shape[0]
    score_scale = HEAD ** (-0.5)
    key_mask = jnp.broadcast_to(allowed[:, None, :], (row_count, group_size, key_count)).reshape(
        row_count * group_size, key_count
    )
    grad_query_list = []
    grad_key_list = []
    grad_value_list = []
    sink_list = []
    for kv_head in range(KV_HEADS):
        low = kv_head * group_size * HEAD
        high = (kv_head + 1) * group_size * HEAD
        query_group = query_rows[:, low:high].reshape(row_count * group_size, HEAD)
        grad_group = grad_rows[:, low:high].reshape(row_count * group_size, HEAD)
        key_group = key_rows[:, kv_head * HEAD : (kv_head + 1) * HEAD]
        value_group = value_rows[:, kv_head * HEAD : (kv_head + 1) * HEAD]
        scores = (
            lax.dot_general(
                query_group, key_group, (((1,), (1,)), ((), ())), preferred_element_type=jnp.float32
            )
            * score_scale
        )
        sink_rows = jnp.tile(sinks[kv_head * group_size : (kv_head + 1) * group_size], row_count)
        row_max = jnp.maximum(jnp.max(jnp.where(key_mask, scores, -jnp.inf), axis=1), sink_rows)
        weights = jnp.where(key_mask, jnp.exp(scores - row_max[:, None]), 0.0)
        row_total = jnp.exp(sink_rows - row_max) + jnp.sum(weights, axis=1)
        log_total = row_max + jnp.log(row_total)
        probabilities = jnp.where(key_mask, jnp.exp(scores - log_total[:, None]), 0.0)
        probs_low = probabilities.astype(jnp.bfloat16)
        attended = jnp.dot(probs_low, value_group, preferred_element_type=jnp.float32).astype(
            jnp.bfloat16
        )
        attended = lax.optimization_barrier(attended)
        row_delta = jnp.sum(grad_group.astype(jnp.float32) * attended.astype(jnp.float32), axis=1)
        grad_prob = lax.dot_general(
            grad_group, value_group, (((1,), (1,)), ((), ())), preferred_element_type=jnp.float32
        )
        dscore = (probabilities * (grad_prob - row_delta[:, None])).astype(jnp.bfloat16)
        grad_query = jnp.dot(dscore, key_group, preferred_element_type=jnp.float32) * score_scale
        grad_query_list.append(grad_query.reshape(row_count, group_size * HEAD))
        grad_key_list.append(
            lax.dot_general(
                dscore, query_group, (((0,), (0,)), ((), ())), preferred_element_type=jnp.float32
            )
            * score_scale
        )
        grad_value_list.append(
            lax.dot_general(
                probs_low, grad_group, (((0,), (0,)), ((), ())), preferred_element_type=jnp.float32
            )
        )
        sink_list.append(
            -jnp.sum(
                (jnp.exp(sink_rows - log_total) * row_delta).reshape(row_count, group_size), axis=0
            )
        )
    return (
        jnp.concatenate(grad_query_list, axis=1),
        jnp.concatenate(grad_key_list, axis=1),
        jnp.concatenate(grad_value_list, axis=1),
        jnp.concatenate(sink_list, axis=0),
    )


def body(queries, keys, values, dout, sinks):
    tok_rows = queries.shape[1]
    ctx_index = lax.axis_index("ctx")
    halo_keys, halo_values = shifted((keys, values), "ctx", 1)
    joined_keys = jnp.concatenate([halo_keys, keys], axis=1)
    joined_values = jnp.concatenate([halo_values, values], axis=1)
    query_pos = ctx_index * tok_rows + jnp.arange(tok_rows, dtype=jnp.int32)
    key_pos = ctx_index * tok_rows - tok_rows + jnp.arange(tok_rows + tok_rows, dtype=jnp.int32)
    allowed = (
        (key_pos[None, :] <= query_pos[:, None])
        & (key_pos[None, :] > query_pos[:, None] - WINDOW)
        & (key_pos[None, :] >= 0)
    )

    def per_sequence(query_rows, key_rows, value_rows, grad_rows):
        return block_terms(query_rows, key_rows, value_rows, grad_rows, sinks, allowed)

    grad_query, grad_key, grad_value, sink_terms = jax.vmap(per_sequence)(
        queries, joined_keys, joined_values, dout
    )
    back_keys, back_values = shifted(
        (as_sent(grad_key[:, :tok_rows]), as_sent(grad_value[:, :tok_rows])), "ctx", -1
    )
    own_keys = grad_key[:, tok_rows:]
    own_values = grad_value[:, tok_rows:]
    own_keys = jnp.concatenate(
        [own_keys[:, : tok_rows - tok_rows], own_keys[:, tok_rows - tok_rows :] + back_keys], axis=1
    )
    own_values = jnp.concatenate(
        [own_values[:, : tok_rows - tok_rows], own_values[:, tok_rows - tok_rows :] + back_values],
        axis=1,
    )
    local_sum = jnp.sum(sink_terms, axis=0)
    sink_total = lax.psum(local_sum, ("dp", "ctx"))
    token_count = lax.axis_size("dp") * queries.shape[0] * lax.axis_size("ctx") * tok_rows
    sink_grad = sink_total / jnp.sqrt(jnp.float32(token_count))
    return (
        grad_query.astype(jnp.bfloat16),
        own_keys.astype(jnp.bfloat16),
        own_values.astype(jnp.bfloat16),
        sink_grad,
    )


def solution(mesh):
    return jax.shard_map(
        body,
        mesh=mesh,
        in_specs=(
            P("dp", "ctx", None),
            P("dp", "ctx", None),
            P("dp", "ctx", None),
            P("dp", "ctx", None),
            P(),
        ),
        out_specs=(P("dp", "ctx", None), P("dp", "ctx", None), P("dp", "ctx", None), P()),
        check_vma=False,
    )
```

profile of v0, /device:TPU:1, one launch (start us, length us, event | category | flops | bytes accessed | tf_op | source)
XLA Modules:
  0.0 170.7 jit_solution(381040747108957759)
XLA Ops:
  0.6 6.8 %collective-permute-start = (bf16[1,128,512]{2,1,0:T(8,128)(2,1)}, bf16[1,128,512]{2,1,0:T(8,128)(2,1)S(1)}, u32[]{:S(2)}, u32[]{:S(2)}) collective-permute-start(bf16[1,128,512]{2,1,0:T(8,128)(2,1)} %param.6), channel_id=1, source_target_pairs={{0,1},{1,2},{2,3},{3,4},{4,5},{5,6},{6,7},{7,8},{8,9},{9,10},{10,1... | collective-permute-start | bytes 393224 | tf_op jit(solution)/shard_map/ppermute | solution.py:15
  7.4 7.7 %collective-permute-start.1 = (bf16[1,128,512]{2,1,0:T(8,128)(2,1)}, bf16[1,128,512]{2,1,0:T(8,128)(2,1)}, u32[]{:S(2)}, u32[]{:S(2)}) collective-permute-start(bf16[1,128,512]{2,1,0:T(8,128)(2,1)} %param.7), channel_id=1, source_target_pairs={{0,1},{1,2},{2,3},{3,4},{4,5},{5,6},{6,7},{7,8},{8,9},{9,10},{10,1... | collective-permute-start | bytes 393224 | tf_op jit(solution)/shard_map/ppermute | solution.py:15
  19.6 0.7 tile.57
  20.4 0.7 reshape.1166
  21.1 0.7 reshape.1167
  21.8 0.7 reshape.1168
  22.5 0.7 reshape.1169
  23.7 0.9 copy-done.26
  26.5 0.7 reduce_sum.138
  27.2 0.7 reduce_max.48
  27.9 0.7 reduce_sum.141
  28.7 0.7 reduce_max.49
  29.4 0.7 reduce_sum.144
  30.2 0.7 reduce_max.50
  30.9 0.7 reduce_max.51
  31.6 0.7 reduce_sum.147
  32.4 0.9 constant_dynamic-update-slice_fusion.3
  34.3 0.7 multiply_reduce_fusion.3
  35.1 1.4 reduce_sum.139
  36.5 0.9 convolution_bitcast_fusion.3
  38.8 0.7 reduce_sum.142
  41.1 0.7 reduce_sum.145
  48.3 0.8 copy-done.21
  50.1 0.7 copy-done.20
  55.6 97.6 %psum.7 = f32[16]{0:T(128)S(1)} all-reduce(f32[16]{0:T(128)S(1)} %maximum_bitcast_fusion), channel_id=1, replica_groups=mesh['dp'=32,'ctx'=16] {'dp','ctx'}, use_global_device_ids=true, to_apply=%region_16.17 | all-reduce | flops 16 | bytes 128 | tf_op jit(solution)/shard_map/psum | solution.py:122
  153.3 1.3 collective-permute-start.3
  154.7 1.3 collective-permute-start.2
  156.3 0.8 pad_maximum_fusion
  157.7 8.7 %collective-permute-done.3 = bf16[1,128,512]{1,2,0:T(8,128)(2,1)S(1)} collective-permute-done((bf16[1,128,512]{1,2,0:T(8,128)(2,1)S(1)}, bf16[1,128,512]{1,2,0:T(8,128)(2,1)S(1)}, u32[]{:S(2)}, u32[]{:S(2)}) %collective-permute-start.3) | collective-permute-done | bytes 131104 | tf_op jit(solution)/shard_map/ppermute | solution.py:15
  166.4 0.8 copy.50
  167.2 2.6 %collective-permute-done.2 = bf16[1,128,512]{1,2,0:T(8,128)(2,1)S(1)} collective-permute-done((bf16[1,128,512]{1,2,0:T(8,128)(2,1)S(1)}, bf16[1,128,512]{1,2,0:T(8,128)(2,1)S(1)}, u32[]{:S(2)}, u32[]{:S(2)}) %collective-permute-start.2) | collective-permute-done | bytes 131104 | tf_op jit(solution)/shard_map/ppermute | solution.py:15
  169.9 0.8 copy.49
  (181 shorter events, 23.7 us)
Async XLA Ops:
  0.6 15.1 %copy-start.12 = (bf16[1,128,2048]{2,1,0:T(8,128)(2,1)S(1)}, bf16[1,128,2048]{2,1,0:T(8,128)(2,1)}, u32[]{:S(2)}) copy-start(bf16[1,128,2048]{2,1,0:T(8,128)(2,1)} %param.5) | copy-start | bytes 1572868
  0.6 23.0 %collective-permute-start = (bf16[1,128,512]{2,1,0:T(8,128)(2,1)}, bf16[1,128,512]{2,1,0:T(8,128)(2,1)S(1)}, u32[]{:S(2)}, u32[]{:S(2)}) collective-permute-start(bf16[1,128,512]{2,1,0:T(8,128)(2,1)} %param.6), channel_id=1, source_target_pairs={{0,1},{1,2},{2,3},{3,4},{4,5},{5,6},{6,7},{7,8},{8,9},{9,10},{10,1... | collective-permute-start | bytes 393224 | tf_op jit(solution)/shard_map/ppermute | solution.py:15
  7.4 25.0 %collective-permute-start.1 = (bf16[1,128,512]{2,1,0:T(8,128)(2,1)}, bf16[1,128,512]{2,1,0:T(8,128)(2,1)}, u32[]{:S(2)}, u32[]{:S(2)}) collective-permute-start(bf16[1,128,512]{2,1,0:T(8,128)(2,1)} %param.7), channel_id=1, source_target_pairs={{0,1},{1,2},{2,3},{3,4},{4,5},{5,6},{6,7},{7,8},{8,9},{9,10},{10,1... | collective-permute-start | bytes 393224 | tf_op jit(solution)/shard_map/ppermute | solution.py:15
  15.7 1.1 copy-start.13
  15.9 8.7 %copy-start.2 = (bf16[512,128]{1,0:T(8,128)(2,1)}, bf16[512,128]{1,0:T(8,128)(2,1)S(1)}, u32[]{:S(2)}) copy-start(bf16[512,128]{1,0:T(8,128)(2,1)S(1)} %reshape.1163) | copy-start | bytes 393220
  16.0 8.9 %copy-start.4 = (bf16[512,128]{1,0:T(8,128)(2,1)}, bf16[512,128]{1,0:T(8,128)(2,1)S(1)}, u32[]{:S(2)}) copy-start(bf16[512,128]{1,0:T(8,128)(2,1)S(1)} %reshape.1159) | copy-start | bytes 393220
  16.1 9.0 %copy-start.6 = (bf16[512,128]{1,0:T(8,128)(2,1)}, bf16[512,128]{1,0:T(8,128)(2,1)S(1)}, u32[]{:S(2)}) copy-start(bf16[512,128]{1,0:T(8,128)(2,1)S(1)} %reshape.1155) | copy-start | bytes 393220
  16.8 8.5 %copy-start = (bf16[512,128]{1,0:T(8,128)(2,1)}, bf16[512,128]{1,0:T(8,128)(2,1)S(1)}, u32[]{:S(2)}) copy-start(bf16[512,128]{1,0:T(8,128)(2,1)S(1)} %reshape.1151) | copy-start | bytes 393220
  17.6 1.3 copy-start.39
  17.6 2.0 %copy-start.37 = (f32[4]{0:T(128)}, f32[4]{0:T(128)S(1)}, u32[]{:S(2)}) copy-start(f32[4]{0:T(128)S(1)} %get-tuple-element.39) | copy-start | bytes 52
  17.6 2.7 %copy-start.35 = (f32[4]{0:T(128)}, f32[4]{0:T(128)S(1)}, u32[]{:S(2)}) copy-start(f32[4]{0:T(128)S(1)} %get-tuple-element.38) | copy-start | bytes 52
  20.4 5.6 %copy-start.29 = (f32[512]{0:T(512)}, f32[512]{0:T(512)S(1)}, u32[]{:S(2)}) copy-start(f32[512]{0:T(512)S(1)} %tile.59) | copy-start | bytes 6148
  23.6 0.9 copy-start.26
  32.4 1.0 copy-start.27
  33.4 1.0 copy-start.11
  36.5 0.9 copy-start.28
  37.7 1.0 copy-start.10
  40.0 1.0 copy-start.9
  42.4 1.0 copy-start.8
  43.9 0.9 copy-start.1
  45.1 0.9 copy-start.7
  46.2 0.9 copy-start.5
  47.4 1.8 %copy-start.42 = (f32[4]{0:T(128)S(1)}, f32[4]{0:T(128)}, u32[]{:S(2)}) copy-start(f32[4]{0:T(128)} %copy-done.41) | copy-start | bytes 52
  48.2 0.9 copy-start.22
  48.2 2.6 %copy-start.40 = (f32[4]{0:T(128)S(1)}, f32[4]{0:T(128)}, u32[]{:S(2)}) copy-start(f32[4]{0:T(128)} %copy-done.39) | copy-start | bytes 52
  49.1 0.9 copy-start.19
  50.0 1.1 copy-start.23
  51.9 0.9 copy-start.16
  54.5 0.9 copy-start.3
  55.4 97.8 %copy-start.14 = (f32[1,256,128]{1,2,0:T(8,128)S(1)}, f32[1,256,128]{1,2,0:T(8,128)}, u32[]{:S(2)}) copy-start(f32[1,256,128]{1,2,0:T(8,128)} %convolution_bitcast_fusion.3) | copy-start | bytes 393220
  153.3 13.1 %collective-permute-start.3 = (bf16[1,128,512]{1,2,0:T(8,128)(2,1)S(1)}, bf16[1,128,512]{1,2,0:T(8,128)(2,1)S(1)}, u32[]{:S(2)}, u32[]{:S(2)}) collective-permute-start(bf16[1,128,512]{1,2,0:T(8,128)(2,1)S(1)} %slice.146), channel_id=1, source_target_pairs={{1,0},{2,1},{3,2},{4,3},{5,4},{6,5},{7,6},{8,7},{9,8},{10,9},{11,1... | collective-permute-start | bytes 393224 | tf_op jit(solution)/shard_map/ppermute | solution.py:15
  154.7 15.2 %collective-permute-start.2 = (bf16[1,128,512]{1,2,0:T(8,128)(2,1)S(1)}, bf16[1,128,512]{1,2,0:T(8,128)(2,1)S(1)}, u32[]{:S(2)}, u32[]{:S(2)}) collective-permute-start(bf16[1,128,512]{1,2,0:T(8,128)(2,1)S(1)} %slice.147), channel_id=1, source_target_pairs={{1,0},{2,1},{3,2},{4,3},{5,4},{6,5},{7,6},{8,7},{9,8},{10,9},{11,1... | collective-permute-start | bytes 393224 | tf_op jit(solution)/shard_map/ppermute | solution.py:15
  (15 other events, 11.2 us)
where the time goes:
time: 172 us; the launch traced here: 171 us
  blocking collectives  97.6 us (57%)
  local copies, waits for them, and re-layouts  31.8 us (18%)
  starting transfers between devices  17 us (10%)
  waiting for transfers between devices  11.4 us (7%)
  matrix products  7.15 us (4%)
  other arithmetic  4.32 us (3%)
    psum x1, blocking collectives, body(): sink_total = lax.psum(local_sum, ('dp', 'ctx'))  97.6 us
    ppermute x4, starting transfers between devices, shifted(): lax.ppermute(value, axis, [(source, source + steps) for source in range(l...  17 us
    unnamed x90, local copies, waits for them, and re-layouts  15.5 us
    ppermute x4, waiting for transfers between devices, shifted(): lax.ppermute(value, axis, [(source, source + steps) for source in range(l...  11.4 us
  transfers between devices with their start and end apart: 4, of which 2 were waited for; matrix products, arithmetic and copies ran while one was open for 10% of the time, Pallas kernels for 0%

commit v1 on v0

v1 whole, which is shorter than its diff:
```python
import functools

import jax
import jax.numpy as jnp
from jax import lax
from jax.experimental import pallas as pl
from jax.experimental.pallas import tpu as pltpu
from jax.sharding import PartitionSpec as P

HEADS = 16
KV_HEADS = 4
GROUP = HEADS // KV_HEADS
HEAD = 128
TOK = 128
SCALE = HEAD ** (-0.5)
LOG2E = 1.4426950408889634
MASKED = -1e30
MESH = pl.DeviceIdType.MESH

NT = (((1,), (1,)), ((), ()))
NN = (((1,), (0,)), ((), ()))
TN = (((0,), (0,)), ((), ()))


def dot(a, b, dims):
    return lax.dot_general(a, b, dims, preferred_element_type=jnp.float32)


def kernel(
    nd, nc, token_root,
    q_hbm, k_hbm, v_hbm, do_hbm, sinks_hbm,
    dq_hbm, dk_hbm, dv_hbm, sg_ref,
    qv, dov, kj, vj, dqv, own, back, landed, outv, bias, sinks_s, terms, part_a, part_b,
    in_sem, kv_sem, sink_sem, halo_send, halo_recv, grad_send, grad_recv, dq_sem, out_sem,
    sum_send, sum_recv,
):
    d = lax.axis_index("dp")
    c = lax.axis_index("ctx")
    right = lax.rem(c + 1, nc)
    left = lax.rem(c + nc - 1, nc)

    def cols(h):
        return pl.ds(h * HEAD, HEAD)

    loads = []
    for g in range(KV_HEADS):
        pairs = [(k_hbm.at[0, :, cols(g)], kj.at[g, pl.ds(TOK, TOK)]), (v_hbm.at[0, :, cols(g)], vj.at[g, pl.ds(TOK, TOK)])]
        loads.append([pltpu.make_async_copy(s, t, kv_sem.at[g, n]) for n, (s, t) in enumerate(pairs)])
        for h in range(g * GROUP, (g + 1) * GROUP):
            loads[g].append(pltpu.make_async_copy(q_hbm.at[0, :, cols(h)], qv.at[h], in_sem.at[0, h]))
            loads[g].append(pltpu.make_async_copy(do_hbm.at[0, :, cols(h)], dov.at[h], in_sem.at[1, h]))
    sink_load = pltpu.make_async_copy(sinks_hbm, sinks_s, sink_sem)
    sink_load.start()
    for group in loads:
        for copy in group:
            copy.start()

    barrier = pltpu.get_barrier_semaphore()
    for step in range(1, nc):
        pl.semaphore_signal(barrier, inc=1, device_id=(d, lax.rem(c + step, nc)), device_id_type=MESH)
    for step in range(1, nd):
        pl.semaphore_signal(barrier, inc=1, device_id=(lax.rem(d + step, nd), c), device_id_type=MESH)
    pl.semaphore_wait(barrier, nc - 1 + nd - 1)

    def remote(src, dst, send, recv, device):
        return pltpu.make_async_remote_copy(
            src_ref=src, dst_ref=dst, send_sem=send, recv_sem=recv, device_id=device, device_id_type=MESH
        )

    halo = []
    for g in range(KV_HEADS):
        for n, (src, dst) in enumerate(((k_hbm, kj), (v_hbm, vj))):
            halo.append(
                remote(src.at[0, :, cols(g)], dst.at[g, pl.ds(0, TOK)], halo_send.at[g, n], halo_recv.at[g, n], (d, right))
            )
            halo[-1].start()

    key = lax.broadcasted_iota(jnp.int32, (TOK, TOK), 0)
    query = lax.broadcasted_iota(jnp.int32, (TOK, TOK), 1)
    first = jnp.where(c == 0, TOK, 0)
    bias[0:TOK] = jnp.where(key > query + first, 0.0, MASKED)
    bias[TOK:] = jnp.where(key <= query, 0.0, MASKED)
    sink_load.wait()

    grads = []
    for g in range(KV_HEADS):
        for copy in loads[g]:
            copy.wait()
        halo[2 * g].wait_recv()
        halo[2 * g + 1].wait_recv()
        heads = pl.ds(g * GROUP, GROUP)
        qs = qv[heads].reshape(GROUP * TOK, HEAD)
        dos = dov[heads].reshape(GROUP * TOK, HEAD)
        kk = kj[g]
        vv = vj[g]
        mask = bias[...]
        mask = jnp.concatenate([mask] * GROUP, axis=1)
        sink = jnp.concatenate(
            [jnp.full((1, TOK), sinks_s[g * GROUP + n] * LOG2E, jnp.float32) for n in range(GROUP)], axis=1
        )
        s = dot(kk, qs, NT) * (SCALE * LOG2E) + mask
        top = jnp.maximum(jnp.max(s, axis=0, keepdims=True), sink)
        e = jnp.exp2(s - top)
        at_sink = jnp.exp2(sink - top)
        inv = 1.0 / (jnp.sum(e, axis=0, keepdims=True) + at_sink)
        p = e * inv
        dp = dot(vv, dos, NT)
        weighted = p * dp
        delta = jnp.sum(weighted, axis=0, keepdims=True)
        term = at_sink * inv * delta
        for n in range(GROUP):
            terms[pl.ds(g * GROUP + n, 1), :] = term[:, n * TOK : (n + 1) * TOK]
        ds = (weighted - p * delta).astype(jnp.bfloat16)
        pr = p.astype(jnp.bfloat16)
        dk = dot(ds, qs, NN) * SCALE
        dv = dot(pr, dos, NN)
        back[0, g] = dk[:TOK].astype(jnp.bfloat16)
        back[1, g] = dv[:TOK].astype(jnp.bfloat16)
        own[0, g] = dk[TOK:]
        own[1, g] = dv[TOK:]
        dq = dot(ds, kk, TN) * SCALE
        dqv[heads] = dq.astype(jnp.bfloat16).reshape(GROUP, TOK, HEAD)
        if g == KV_HEADS - 1:
            row = lax.broadcasted_iota(jnp.int32, (HEADS, TOK), 0)
            lane = lax.broadcasted_iota(jnp.int32, (HEADS, TOK), 1)
            sums = jnp.sum(terms[...], axis=1, keepdims=True)
            part_a[d] = jnp.sum(jnp.where(row == lane, sums, 0.0), axis=0, keepdims=True)
            stage_a = [
                remote(part_a.at[d], part_a.at[d], sum_send.at[0], sum_recv.at[0], (lax.rem(d + step, nd), c))
                for step in range(1, nd)
            ]
            for copy in stage_a:
                copy.start()
        for n in range(2):
            copy = remote(back.at[n, g], landed.at[n, g], grad_send.at[g, n], grad_recv.at[g, n], (d, left))
            copy.start()
            grads.append(copy)
        for h in range(g * GROUP, (g + 1) * GROUP):
            pltpu.make_async_copy(dqv.at[h], dq_hbm.at[0, :, cols(h)], dq_sem.at[h]).start()

    remote(part_a.at[pl.ds(0, nd - 1)], part_a.at[pl.ds(0, nd - 1)], sum_send.at[0], sum_recv.at[0], (d, left)).wait_recv()
    part_b[c] = jnp.sum(part_a[...], axis=0)
    for step in range(1, nc):
        remote(part_b.at[c], part_b.at[c], sum_send.at[1], sum_recv.at[1], (d, lax.rem(c + step, nc))).start()

    for g in range(KV_HEADS):
        for n, out in enumerate((dk_hbm, dv_hbm)):
            grads[2 * g + n].wait_recv()
            outv[n, g] = (own[n, g] + landed[n, g].astype(jnp.float32)).astype(jnp.bfloat16)
            pltpu.make_async_copy(outv.at[n, g], out.at[0, :, cols(g)], out_sem.at[g, n]).start()

    remote(part_b.at[pl.ds(0, nc - 1)], part_b.at[pl.ds(0, nc - 1)], sum_send.at[1], sum_recv.at[1], (d, left)).wait_recv()
    sg_ref[...] = jnp.sum(part_b[...], axis=0) * (-1.0 / token_root)

    for copy in halo + grads:
        copy.wait_send()
    remote(part_a.at[pl.ds(0, nd - 1)], part_a.at[pl.ds(0, nd - 1)], sum_send.at[0], sum_recv.at[0], (d, left)).wait_send()
    remote(part_b.at[pl.ds(0, nc - 1)], part_b.at[pl.ds(0, nc - 1)], sum_send.at[1], sum_recv.at[1], (d, left)).wait_send()
    for h in range(HEADS):
        pltpu.make_async_copy(dqv.at[h], dq_hbm.at[0, :, cols(h)], dq_sem.at[h]).wait()
    for g in range(KV_HEADS):
        for n, out in enumerate((dk_hbm, dv_hbm)):
            pltpu.make_async_copy(outv.at[n, g], out.at[0, :, cols(g)], out_sem.at[g, n]).wait()


def solution(mesh):
    nd, nc = mesh.shape["dp"], mesh.shape["ctx"]
    any_space = pl.BlockSpec(memory_space=pl.ANY)

    def body(queries, keys, values, dout, sinks):
        token_root = float(nd * queries.shape[0] * nc * queries.shape[1]) ** 0.5
        bf16, f32 = jnp.bfloat16, jnp.float32
        dq, dk, dv, sg = pl.pallas_call(
            functools.partial(kernel, nd, nc, token_root),
            out_shape=(
                jax.ShapeDtypeStruct(queries.shape, bf16),
                jax.ShapeDtypeStruct(keys.shape, bf16),
                jax.ShapeDtypeStruct(values.shape, bf16),
                jax.ShapeDtypeStruct((1, HEAD), f32),
            ),
            in_specs=[any_space] * 5,
            out_specs=(any_space, any_space, any_space, pl.BlockSpec(memory_space=pltpu.VMEM)),
            scratch_shapes=[
                pltpu.VMEM((HEADS, TOK, HEAD), bf16),
                pltpu.VMEM((HEADS, TOK, HEAD), bf16),
                pltpu.VMEM((KV_HEADS, 2 * TOK, HEAD), bf16),
                pltpu.VMEM((KV_HEADS, 2 * TOK, HEAD), bf16),
                pltpu.VMEM((HEADS, TOK, HEAD), bf16),
                pltpu.VMEM((2, KV_HEADS, TOK, HEAD), f32),
                pltpu.VMEM((2, KV_HEADS, TOK, HEAD), bf16),
                pltpu.VMEM((2, KV_HEADS, TOK, HEAD), bf16),
                pltpu.VMEM((2, KV_HEADS, TOK, HEAD), bf16),
                pltpu.VMEM((2 * TOK, TOK), f32),
                pltpu.SMEM((HEADS,), f32),
                pltpu.VMEM((HEADS, TOK), f32),
                pltpu.VMEM((nd, 1, HEAD), f32),
                pltpu.VMEM((nc, 1, HEAD), f32),
                pltpu.SemaphoreType.DMA((2, HEADS)),
                pltpu.SemaphoreType.DMA((KV_HEADS, 2)),
                pltpu.SemaphoreType.DMA,
                pltpu.SemaphoreType.DMA((KV_HEADS, 2)),
                pltpu.SemaphoreType.DMA((KV_HEADS, 2)),
                pltpu.SemaphoreType.DMA((KV_HEADS, 2)),
                pltpu.SemaphoreType.DMA((KV_HEADS, 2)),
                pltpu.SemaphoreType.DMA((HEADS,)),
                pltpu.SemaphoreType.DMA((KV_HEADS, 2)),
                pltpu.SemaphoreType.DMA((2,)),
                pltpu.SemaphoreType.DMA((2,)),
            ],
            compiler_params=pltpu.CompilerParams(collective_id=0, has_side_effects=True),
        )(queries, keys, values, dout, sinks)
        return dq, dk, dv, sg[0, :HEADS]

    tokens = P("dp", "ctx", None)
    return jax.shard_map(
        body,
        mesh=mesh,
        in_specs=(tokens, tokens, tokens, tokens, P()),
        out_specs=(tokens, tokens, tokens, P()),
        check_vma=False,
    )
```

time: 172 us -> 48.5 us (0.28)
  blocking collectives: 97.6 us -> 0 us
  Pallas kernels: 0 us -> 43.1 us
  local copies, waits for them, and re-layouts: 31.8 us -> 4.65 us
  starting transfers between devices: 17 us -> 0 us
  waiting for transfers between devices: 11.4 us -> 0 us
  matrix products: 7.15 us -> 0 us
  other arithmetic: 4.32 us -> 0 us
    psum x1 -> x0, blocking collectives: 97.6 us -> none  [body(): sink_total = lax.psum(local_sum, ('dp', 'ctx'))]
    pallas_call x0 -> x1, Pallas kernels: none -> 43.1 us  [body(): pl.pallas_call(functools.partial(kernel, nd, nc, token_root), out_shape=(...]
    ppermute x4 -> x0, starting transfers between devices: 17 us -> none  [shifted(): lax.ppermute(value, axis, [(source, source + steps) for source in range(l...]
    ppermute x4 -> x0, waiting for transfers between devices: 11.4 us -> none  [shifted(): lax.ppermute(value, axis, [(source, source + steps) for source in range(l...]
    unnamed x90 -> x9, local copies, waits for them, and re-layouts: 15.5 us -> 4.14 us
    dot_general x24 -> x0, matrix products: 7.15 us -> none  [the longest x4 1.73 us: block_terms(): lax.dot_general(probs_low, grad_group, (((0,), (0,)), ((), ())), preferre...]
    reduce_sum x16 -> x0, local copies, waits for them, and re-layouts: 6.41 us -> none  [the longest x8 3.21 us: block_terms(): jnp.sum(grad_group.astype(jnp.float32) * attended.astype(jnp.float32), ax...]
    reduce_max x8 -> x0, local copies, waits for them, and re-layouts: 3.17 us -> none  [block_terms(): jnp.max(jnp.where(key_mask, scores, -jnp.inf), axis=1)]
  transfers between devices with their start and end apart: 4 -> 0, of which waited for: 2 -> 0; matrix products, arithmetic and copies ran while one was open for 10% -> 0% of each run, Pallas kernels for 0% -> 0%
where the time goes in v1:
time: 48.5 us; the launch traced here: 48.4 us
  Pallas kernels  43.1 us (89%)
  local copies, waits for them, and re-layouts  4.65 us (10%)
  between operations  0.65 us (1%)
    pallas_call x1, Pallas kernels, body(): pl.pallas_call(functools.partial(kernel, nd, nc, token_root), out_shape=(...  43.1 us
    unnamed x9, local copies, waits for them, and re-layouts  4.14 us

profile of v1, /device:TPU:1, one launch (start us, length us, event | category | flops | bytes accessed | tf_op | source)
XLA Modules:
  0.0 48.4 jit_solution(9509082808956409157)
XLA Ops:
  0.6 43.1 %shard_map.84 = (bf16[1,128,2048]{2,1,0:T(8,128)(2,1)}, bf16[1,128,512]{2,1,0:T(8,128)(2,1)}, bf16[1,128,512]{2,1,0:T(8,128)(2,1)}, f32[1,128]{1,0:T(1,128)}) custom-call(bf16[1,128,2048]{2,1,0:T(8,128)(2,1)} %q_hbm.1, bf16[1,128,512]{2,1,0:T(8,128)(2,1)} %k_hbm.1, bf16[1,128,512]{2,1,0:T(8,128)(2,1)} %v_hbm.1, bf16[1,128,2048]{2,1,0:T(8,128)(2,1)} %do_hbm.1, ...), custom_call_target="tpu_custom_call" | custom-call | tf_op jit(solution)/shard_map/pallas_call | solution.py:173
  43.7 0.0 copy-start.2
  43.7 0.6 %copy-done.2 = f32[1,128]{1,0:T(1,128)S(1)} copy-done((f32[1,128]{1,0:T(1,128)S(1)}, f32[1,128]{1,0:T(1,128)}, u32[]{:S(2)}) %copy-start.2) | copy-done | bytes 536
  44.3 0.5 %slice_bitcast_fusion = f32[16]{0:T(128)} fusion(f32[1,128]{1,0:T(1,128)S(1)} %copy-done.2), kind=kLoop, calls=%fused_computation | loop fusion | bytes 128 | tf_op jit(solution)/shard_map/squeeze | solution.py:212
  44.9 0.0 copy-start.1
  44.9 1.9 %copy.12 = bf16[1,128,2048]{2,1,0:T(8,128)(2,1)} copy(bf16[1,128,2048]{2,1,0:T(8,128)(2,1)} %get-tuple-element.16) | data formatting | bytes 1048576
  46.8 0.0 copy-done.1
  46.8 0.0 copy-start
  46.8 0.7 %copy.13 = bf16[1,128,512]{2,1,0:T(8,128)(2,1)} copy(bf16[1,128,512]{2,1,0:T(8,128)(2,1)S(1)} %copy-done.1) | data formatting | bytes 262144
  47.4 0.3 copy-done
  47.7 0.7 %copy.14 = bf16[1,128,512]{2,1,0:T(8,128)(2,1)} copy(bf16[1,128,512]{2,1,0:T(8,128)(2,1)S(1)} %copy-done) | data formatting | bytes 262144
Async XLA Ops:
  43.7 0.6 %copy-start.2 = (f32[1,128]{1,0:T(1,128)S(1)}, f32[1,128]{1,0:T(1,128)}, u32[]{:S(2)}) copy-start(f32[1,128]{1,0:T(1,128)} %get-tuple-element.11) | copy-start | bytes 1540
  44.9 1.9 %copy-start.1 = (bf16[1,128,512]{2,1,0:T(8,128)(2,1)S(1)}, bf16[1,128,512]{2,1,0:T(8,128)(2,1)}, u32[]{:S(2)}) copy-start(bf16[1,128,512]{2,1,0:T(8,128)(2,1)} %get-tuple-element.17) | copy-start | bytes 393220
  46.8 1.0 %copy-start = (bf16[1,128,512]{2,1,0:T(8,128)(2,1)S(1)}, bf16[1,128,512]{2,1,0:T(8,128)(2,1)}, u32[]{:S(2)}) copy-start(bf16[1,128,512]{2,1,0:T(8,128)(2,1)} %get-tuple-element.18) | copy-start | bytes 393220

commit v2 on v1

v2 whole, which is shorter than its diff:
```python
import functools

import jax
import jax.numpy as jnp
from jax import lax
from jax.experimental import pallas as pl
from jax.experimental.pallas import tpu as pltpu
from jax.sharding import PartitionSpec as P

HEADS = 16
KV_HEADS = 4
GROUP = HEADS // KV_HEADS
HEAD = 128
TOK = 128
SCALE = HEAD ** (-0.5)
LOG2E = 1.4426950408889634
MASKED = -1e30
MESH = pl.DeviceIdType.MESH

NT = (((1,), (1,)), ((), ()))
NN = (((1,), (0,)), ((), ()))
TN = (((0,), (0,)), ((), ()))


def dot(a, b, dims):
    return lax.dot_general(a, b, dims, preferred_element_type=jnp.float32)


def remote(src, dst, send, recv, device):
    return pltpu.make_async_remote_copy(
        src_ref=src, dst_ref=dst, send_sem=send, recv_sem=recv, device_id=device, device_id_type=MESH
    )


def cols(h):
    return pl.ds(h * HEAD, HEAD)


def kernel(
    nd, nc, token_root,
    q_hbm, k_hbm, v_hbm, do_hbm, sinks_hbm,
    dq_ref, dk_ref, dv_ref, sg_ref,
    qv, dov, kj, vj, own, back, landed, bias, sinks_s, terms, part_a, part_b,
    in_sem, kv_sem, sink_sem, halo_send, halo_recv, grad_send, grad_recv, sum_send, sum_recv,
):
    d = lax.axis_index("dp")
    c = lax.axis_index("ctx")
    left, right = c - 1, c + 1
    has_left, has_right = c > 0, c < nc - 1

    x_n, y_n, z_n = nc // 4, nd // 4, 8
    x, y, core = c // 4, d // 4, d % 2
    z = (c % 4) * 2 + (d // 2) % 2

    def at(dx, dy, dz, dcore):
        to_x, to_y, to_z, to_core = (x + dx) % x_n, (y + dy) % y_n, (z + dz) % z_n, (core + dcore) % 2
        return to_y * 4 + (to_z % 2) * 2 + to_core, to_x * 4 + to_z // 2

    def hops(n, step):
        return min(step, n - step)

    stage_a = [(0, 0, dz, dcore) for dz in range(z_n) for dcore in range(2)][1:]
    stage_b = [(dx, dy, 0, 0) for dx in range(x_n) for dy in range(y_n)][1:]
    stage_a.sort(key=lambda o: -hops(z_n, o[2]))
    stage_b.sort(key=lambda o: -hops(x_n, o[0]) - hops(y_n, o[1]))

    loads = []
    for g in range(KV_HEADS):
        pairs = [(k_hbm.at[0, :, cols(g)], kj.at[g, pl.ds(TOK, TOK)]), (v_hbm.at[0, :, cols(g)], vj.at[g, pl.ds(TOK, TOK)])]
        loads.append([pltpu.make_async_copy(s, t, kv_sem.at[g, n]) for n, (s, t) in enumerate(pairs)])
        for h in range(g * GROUP, (g + 1) * GROUP):
            loads[g].append(pltpu.make_async_copy(q_hbm.at[0, :, cols(h)], qv.at[h], in_sem.at[0, h]))
            loads[g].append(pltpu.make_async_copy(do_hbm.at[0, :, cols(h)], dov.at[h], in_sem.at[1, h]))
    sink_load = pltpu.make_async_copy(sinks_hbm, sinks_s, sink_sem)
    sink_load.start()
    for group in loads:
        for copy in group:
            copy.start()

    barrier = pltpu.get_barrier_semaphore()

    def greet(device):
        pl.semaphore_signal(barrier, inc=1, device_id=device, device_id_type=MESH)

    @pl.when(has_left)
    def _():
        greet((d, left))

    @pl.when(has_right)
    def _():
        greet((d, right))

    for offset in stage_a + stage_b:
        greet(at(*offset))
    as_int = lambda flag: jnp.where(flag, 1, 0)
    pl.semaphore_wait(barrier, as_int(has_left) + as_int(has_right) + len(stage_a) + len(stage_b))

    halo = []
    for g in range(KV_HEADS):
        for n, (src, dst) in enumerate(((k_hbm, kj), (v_hbm, vj))):
            halo.append(
                remote(src.at[0, :, cols(g)], dst.at[g, pl.ds(0, TOK)], halo_send.at[g, n], halo_recv.at[g, n], (d, right))
            )

    @pl.when(has_right)
    def _():
        for copy in halo:
            copy.start()

    @pl.when(c == 0)
    def _():
        kj[:, 0:TOK] = jnp.zeros((KV_HEADS, TOK, HEAD), jnp.bfloat16)
        vj[:, 0:TOK] = jnp.zeros((KV_HEADS, TOK, HEAD), jnp.bfloat16)

    key = lax.broadcasted_iota(jnp.int32, (TOK, TOK), 0)
    query = lax.broadcasted_iota(jnp.int32, (TOK, TOK), 1)
    first = jnp.where(c == 0, TOK, 0)
    bias[0:TOK] = jnp.where(key > query + first, 0.0, MASKED)
    bias[TOK:] = jnp.where(key <= query, 0.0, MASKED)
    sink_load.wait()

    def sum_stage(n, part, slot, offsets, value):
        part[slot] = value
        for offset in offsets:
            remote(part.at[slot], part.at[slot], sum_send.at[n], sum_recv.at[n], at(*offset)).start()
        if offsets:
            some = part.at[pl.ds(0, len(offsets))]
            return [remote(some, some, sum_send.at[n], sum_recv.at[n], at(*offsets[0]))]
        return []

    grads = []
    for g in range(KV_HEADS):
        for copy in loads[g]:
            copy.wait()

        @pl.when(has_left)
        def _():
            halo[2 * g].wait_recv()
            halo[2 * g + 1].wait_recv()

        heads = pl.ds(g * GROUP, GROUP)
        qs = qv[heads].reshape(GROUP * TOK, HEAD)
        dos = dov[heads].reshape(GROUP * TOK, HEAD)
        kk = kj[g]
        vv = vj[g]
        mask = bias[...]
        mask = jnp.concatenate([mask] * GROUP, axis=1)
        sink = jnp.concatenate(
            [jnp.full((1, TOK), sinks_s[g * GROUP + n] * LOG2E, jnp.float32) for n in range(GROUP)], axis=1
        )
        s = dot(kk, qs, NT) * (SCALE * LOG2E) + mask
        top = jnp.maximum(jnp.max(s, axis=0, keepdims=True), sink)
        e = jnp.exp2(s - top)
        at_sink = jnp.exp2(sink - top)
        inv = 1.0 / (jnp.sum(e, axis=0, keepdims=True) + at_sink)
        p = e * inv
        dp = dot(vv, dos, NT)
        weighted = p * dp
        delta = jnp.sum(weighted, axis=0, keepdims=True)
        term = at_sink * inv * delta
        for n in range(GROUP):
            terms[pl.ds(g * GROUP + n, 1), :] = term[:, n * TOK : (n + 1) * TOK]
        if g == KV_HEADS - 1:
            row = lax.broadcasted_iota(jnp.int32, (HEADS, TOK), 0)
            lane = lax.broadcasted_iota(jnp.int32, (HEADS, TOK), 1)
            sums = jnp.sum(terms[...], axis=1, keepdims=True)
            local = jnp.sum(jnp.where(row == lane, sums, 0.0), axis=0, keepdims=True)
            sent_a = sum_stage(0, part_a, z * 2 + core, stage_a, local)

        ds = (weighted - p * delta).astype(jnp.bfloat16)
        pr = p.astype(jnp.bfloat16)
        dk = dot(ds, qs, NN) * SCALE
        dv = dot(pr, dos, NN)
        back[0, g] = dk[:TOK].astype(jnp.bfloat16)
        back[1, g] = dv[:TOK].astype(jnp.bfloat16)
        own[0, g] = dk[TOK:]
        own[1, g] = dv[TOK:]
        dq = (dot(ds, kk, TN) * SCALE).astype(jnp.bfloat16)
        for n in range(GROUP):
            dq_ref[0, :, cols(g * GROUP + n)] = dq[n * TOK : (n + 1) * TOK]
        for n in range(2):
            grads.append(remote(back.at[n, g], landed.at[n, g], grad_send.at[g, n], grad_recv.at[g, n], (d, left)))

        @pl.when(has_left)
        def _():
            for copy in grads[2 * g :]:
                copy.start()

    for copy in sent_a:
        copy.wait_recv()
    sent_b = sum_stage(1, part_b, x * y_n + y, stage_b, jnp.sum(part_a[...], axis=0))

    for g in range(KV_HEADS):
        for n, out in enumerate((dk_ref, dv_ref)):

            @pl.when(has_right)
            def _():
                grads[2 * g + n].wait_recv()
                out[0, :, cols(g)] = (own[n, g] + landed[n, g].astype(jnp.float32)).astype(jnp.bfloat16)

            @pl.when(c == nc - 1)
            def _():
                out[0, :, cols(g)] = own[n, g].astype(jnp.bfloat16)

    for copy in sent_b:
        copy.wait_recv()
    sg_ref[...] = jnp.sum(part_b[...], axis=0) * (-1.0 / token_root)

    @pl.when(has_right)
    def _():
        for copy in halo:
            copy.wait_send()

    @pl.when(has_left)
    def _():
        for copy in grads:
            copy.wait_send()

    for copy in sent_a + sent_b:
        copy.wait_send()


def write_kernel(dq_ref, dk_ref, dv_ref, sg_ref, dq_out, dk_out, dv_out, sg_out, sem):
    pairs = ((dq_ref, dq_out), (dk_ref, dk_out), (dv_ref, dv_out))
    copies = [pltpu.make_async_copy(src, dst, sem.at[n]) for n, (src, dst) in enumerate(pairs)]
    for copy in copies:
        copy.start()
    sg_out[...] = sg_ref[0, :HEADS]
    for copy in copies:
        copy.wait()


def solution(mesh):
    nd, nc = mesh.shape["dp"], mesh.shape["ctx"]
    any_space = pl.BlockSpec(memory_space=pl.ANY)
    vmem_space = pl.BlockSpec(memory_space=pltpu.VMEM)

    def body(queries, keys, values, dout, sinks):
        token_root = float(nd * queries.shape[0] * nc * queries.shape[1]) ** 0.5
        bf16, f32 = jnp.bfloat16, jnp.float32
        results = pl.pallas_call(
            functools.partial(kernel, nd, nc, token_root),
            out_shape=(
                pltpu.VMEM(queries.shape, bf16),
                pltpu.VMEM(keys.shape, bf16),
                pltpu.VMEM(values.shape, bf16),
                pltpu.VMEM((1, HEAD), f32),
            ),
            in_specs=[any_space] * 5,
            out_specs=(vmem_space,) * 4,
            scratch_shapes=[
                pltpu.VMEM((HEADS, TOK, HEAD), bf16),
                pltpu.VMEM((HEADS, TOK, HEAD), bf16),
                pltpu.VMEM((KV_HEADS, 2 * TOK, HEAD), bf16),
                pltpu.VMEM((KV_HEADS, 2 * TOK, HEAD), bf16),
                pltpu.VMEM((2, KV_HEADS, TOK, HEAD), f32),
                pltpu.VMEM((2, KV_HEADS, TOK, HEAD), bf16),
                pltpu.VMEM((2, KV_HEADS, TOK, HEAD), bf16),
                pltpu.VMEM((2 * TOK, TOK), f32),
                pltpu.SMEM((HEADS,), f32),
                pltpu.VMEM((HEADS, TOK), f32),
                pltpu.VMEM((16, 1, HEAD), f32),
                pltpu.VMEM((nd * nc // 16, 1, HEAD), f32),
                pltpu.SemaphoreType.DMA((2, HEADS)),
                pltpu.SemaphoreType.DMA((KV_HEADS, 2)),
                pltpu.SemaphoreType.DMA,
                pltpu.SemaphoreType.DMA((KV_HEADS, 2)),
                pltpu.SemaphoreType.DMA((KV_HEADS, 2)),
                pltpu.SemaphoreType.DMA((KV_HEADS, 2)),
                pltpu.SemaphoreType.DMA((KV_HEADS, 2)),
                pltpu.SemaphoreType.DMA((2,)),
                pltpu.SemaphoreType.DMA((2,)),
            ],
            compiler_params=pltpu.CompilerParams(collective_id=0, has_side_effects=True),
        )(queries, keys, values, dout, sinks)
        return pl.pallas_call(
            write_kernel,
            out_shape=(
                jax.ShapeDtypeStruct(queries.shape, bf16),
                jax.ShapeDtypeStruct(keys.shape, bf16),
                jax.ShapeDtypeStruct(values.shape, bf16),
                jax.ShapeDtypeStruct((HEADS,), f32),
            ),
            in_specs=[vmem_space] * 4,
            out_specs=(any_space, any_space, any_space, vmem_space),
            scratch_shapes=[pltpu.SemaphoreType.DMA((3,))],
            compiler_params=pltpu.CompilerParams(vmem_limit_bytes=1 << 20),
        )(*results)

    tokens = P("dp", "ctx", None)
    return jax.shard_map(
        body,
        mesh=mesh,
        in_specs=(tokens, tokens, tokens, tokens, P()),
        out_specs=(tokens, tokens, tokens, P()),
        check_vma=False,
    )
```

time: 48.5 us -> 43.7 us (0.901)
  local copies, waits for them, and re-layouts: 4.65 us -> 0 us
    unnamed x9 -> x0, local copies, waits for them, and re-layouts: 4.14 us -> none
    pallas_call x1, Pallas kernels: 43.1 us -> 41.6 us  [body(): pl.pallas_call(functools.partial(kernel, nd, nc, token_root), out_shape=(...]
    pallas_call x0 -> x1, Pallas kernels: none -> 1.41 us  [body(): pl.pallas_call(write_kernel, out_shape=(jax.ShapeDtypeStruct(queries.shap...]
    squeeze x1 -> x0, local copies, waits for them, and re-layouts: 0.51 us -> none  [body(): return (dq, dk, dv, sg[0, :HEADS])]
where the time goes in v2:
time: 43.7 us; the launch traced here: 43.6 us
  Pallas kernels  43 us (98%)
  between operations  0.64 us (1%)
    pallas_call x1, Pallas kernels, body(): pl.pallas_call(functools.partial(kernel, nd, nc, token_root), out_shape=(...  41.6 us
    pallas_call x1, Pallas kernels, body(): pl.pallas_call(write_kernel, out_shape=(jax.ShapeDtypeStruct(queries.shap...  1.41 us

profile of v2, /device:TPU:1, one launch (start us, length us, event | category | flops | bytes accessed | tf_op | source)
XLA Modules:
  0.0 43.6 jit_solution(1265998593884828392)
XLA Ops:
  0.6 41.6 %shard_map.84 = (bf16[1,128,2048]{2,1,0:T(8,128)(2,1)S(1)}, bf16[1,128,512]{2,1,0:T(8,128)(2,1)S(1)}, bf16[1,128,512]{2,1,0:T(8,128)(2,1)S(1)}, f32[1,128]{1,0:T(1,128)S(1)}) custom-call(bf16[1,128,2048]{2,1,0:T(8,128)(2,1)} %q_hbm.1, bf16[1,128,512]{2,1,0:T(8,128)(2,1)} %k_hbm.1, bf16[1,128,512]{2,1,0:T(8,128)(2,1)} %v_hbm.1, bf16[1,128,2048]{2,1,0:T(8,128)(2,1)} %do_hbm.1, ...), custom_call_target="tpu_custom_call" | custom-call | tf_op jit(solution)/shard_map/pallas_call | solution.py:241
  42.2 1.4 %shard_map.85 = (bf16[1,128,2048]{2,1,0:T(8,128)(2,1)}, bf16[1,128,512]{2,1,0:T(8,128)(2,1)}, bf16[1,128,512]{2,1,0:T(8,128)(2,1)}, f32[16]{0:T(128)}) custom-call(bf16[1,128,2048]{2,1,0:T(8,128)(2,1)S(1)} %get-tuple-element.8.dq_ref, bf16[1,128,512]{2,1,0:T(8,128)(2,1)S(1)} %get-tuple-element.9.dk_ref, bf16[1,128,512]{2,1,0:T(8,128)(2,1)S(1)} %get-tuple-element.10.dv_ref, ...), custom_call_target="tpu_custom_call" | custom-call | tf_op jit(solution)/shard_map/pallas_call | solution.py:276

commit v3 on v2

--- a/solution.py
+++ b/solution.py
@@ -40,7 +40,7 @@
     nd, nc, token_root,
     q_hbm, k_hbm, v_hbm, do_hbm, sinks_hbm,
     dq_ref, dk_ref, dv_ref, sg_ref,
-    qv, dov, kj, vj, own, back, landed, bias, sinks_s, terms, part_a, part_b,
+    qv, dov, kv, prior, own, back, landed, bias, sinks_s, terms, part_a, part_b,
     in_sem, kv_sem, sink_sem, halo_send, halo_recv, grad_send, grad_recv, sum_send, sum_recv,
 ):
     d = lax.axis_index("dp")
@@ -59,23 +59,11 @@
     def hops(n, step):
         return min(step, n - step)
 
-    stage_a = [(0, 0, dz, dcore) for dz in range(z_n) for dcore in range(2)][1:]
-    stage_b = [(dx, dy, 0, 0) for dx in range(x_n) for dy in range(y_n)][1:]
-    stage_a.sort(key=lambda o: -hops(z_n, o[2]))
-    stage_b.sort(key=lambda o: -hops(x_n, o[0]) - hops(y_n, o[1]))
-
-    loads = []
-    for g in range(KV_HEADS):
-        pairs = [(k_hbm.at[0, :, cols(g)], kj.at[g, pl.ds(TOK, TOK)]), (v_hbm.at[0, :, cols(g)], vj.at[g, pl.ds(TOK, TOK)])]
-        loads.append([pltpu.make_async_copy(s, t, kv_sem.at[g, n]) for n, (s, t) in enumerate(pairs)])
-        for h in range(g * GROUP, (g + 1) * GROUP):
-            loads[g].append(pltpu.make_async_copy(q_hbm.at[0, :, cols(h)], qv.at[h], in_sem.at[0, h]))
-            loads[g].append(pltpu.make_async_copy(do_hbm.at[0, :, cols(h)], dov.at[h], in_sem.at[1, h]))
-    sink_load = pltpu.make_async_copy(sinks_hbm, sinks_s, sink_sem)
-    sink_load.start()
-    for group in loads:
-        for copy in group:
-            copy.start()
+    stage_a = [(dx, 0, 0, dc) for dx in range(x_n) for dc in range(2)][1:]
+    stage_b = [(0, dy, dz, 0) for dy in range(y_n) for dz in range(z_n)][1:]
+    far = lambda o: -hops(x_n, o[0]) - hops(y_n, o[1]) - hops(z_n, o[2])
+    stage_a.sort(key=far)
+    stage_b.sort(key=far)
 
     barrier = pltpu.get_barrier_semaphore()
 
@@ -92,14 +80,27 @@
 
     for offset in stage_a + stage_b:
         greet(at(*offset))
+
+    sink_load = pltpu.make_async_copy(sinks_hbm, sinks_s, sink_sem)
+    own_loads = [pltpu.make_async_copy(src.at[0], dst, kv_sem.at[n]) for n, (src, dst) in enumerate(((k_hbm, kv.at[0]), (v_hbm, kv.at[1])))]
+    loads = [
+        [
+            pltpu.make_async_copy(src.at[0, :, pl.ds(g * GROUP * HEAD, GROUP * HEAD)], dst.at[g], in_sem.at[n, g])
+            for n, (src, dst) in enumerate(((q_hbm, qv), (do_hbm, dov)))
+        ]
+        for g in range(KV_HEADS)
+    ]
+    for copy in [sink_load, *own_loads, *sum(loads, [])]:
+        copy.start()
+
     as_int = lambda flag: jnp.where(flag, 1, 0)
     pl.semaphore_wait(barrier, as_int(has_left) + as_int(has_right) + len(stage_a) + len(stage_b))
 
     halo = []
     for g in range(KV_HEADS):
-        for n, (src, dst) in enumerate(((k_hbm, kj), (v_hbm, vj))):
+        for n, src in enumerate((k_hbm, v_hbm)):
             halo.append(
-                remote(src.at[0, :, cols(g)], dst.at[g, pl.ds(0, TOK)], halo_send.at[g, n], halo_recv.at[g, n], (d, right))
+                remote(src.at[0, :, cols(g)], prior.at[n, g], halo_send.at[g, n], halo_recv.at[g, n], (d, right))
             )
 
     @pl.when(has_right)
@@ -109,15 +110,15 @@
 
     @pl.when(c == 0)
     def _():
-        kj[:, 0:TOK] = jnp.zeros((KV_HEADS, TOK, HEAD), jnp.bfloat16)
-        vj[:, 0:TOK] = jnp.zeros((KV_HEADS, TOK, HEAD), jnp.bfloat16)
+        prior[...] = jnp.zeros((2, KV_HEADS, TOK, HEAD), jnp.bfloat16)
 
     key = lax.broadcasted_iota(jnp.int32, (TOK, TOK), 0)
     query = lax.broadcasted_iota(jnp.int32, (TOK, TOK), 1)
     first = jnp.where(c == 0, TOK, 0)
     bias[0:TOK] = jnp.where(key > query + first, 0.0, MASKED)
     bias[TOK:] = jnp.where(key <= query, 0.0, MASKED)
-    sink_load.wait()
+    for copy in [sink_load, *own_loads]:
+        copy.wait()
 
     def sum_stage(n, part, slot, offsets, value):
         part[slot] = value
@@ -133,16 +134,19 @@
         for copy in loads[g]:
             copy.wait()
 
-        @pl.when(has_left)
-        def _():
-            halo[2 * g].wait_recv()
-            halo[2 * g + 1].wait_recv()
-
-        heads = pl.ds(g * GROUP, GROUP)
-        qs = qv[heads].reshape(GROUP * TOK, HEAD)
-        dos = dov[heads].reshape(GROUP * TOK, HEAD)
-        kk = kj[g]
-        vv = vj[g]
+        def stacked(ref):
+            return jnp.concatenate([ref[g, :, cols(n)] for n in range(GROUP)], axis=0)
+
+        def joined(n):
+            @pl.when(has_left)
+            def _():
+                halo[2 * g + n].wait_recv()
+
+            return jnp.concatenate([prior[n, g], kv[n, :, cols(g)]], axis=0)
+
+        qs = stacked(qv)
+        dos = stacked(dov)
+        kk = joined(0)
         mask = bias[...]
         mask = jnp.concatenate([mask] * GROUP, axis=1)
         sink = jnp.concatenate(
@@ -154,6 +158,7 @@
         at_sink = jnp.exp2(sink - top)
         inv = 1.0 / (jnp.sum(e, axis=0, keepdims=True) + at_sink)
         p = e * inv
+        vv = joined(1)
         dp = dot(vv, dos, NT)
         weighted = p * dp
         delta = jnp.sum(weighted, axis=0, keepdims=True)
@@ -165,7 +170,7 @@
             lane = lax.broadcasted_iota(jnp.int32, (HEADS, TOK), 1)
             sums = jnp.sum(terms[...], axis=1, keepdims=True)
             local = jnp.sum(jnp.where(row == lane, sums, 0.0), axis=0, keepdims=True)
-            sent_a = sum_stage(0, part_a, z * 2 + core, stage_a, local)
+            sent_a = sum_stage(0, part_a, x * 2 + core, stage_a, local)
 
         ds = (weighted - p * delta).astype(jnp.bfloat16)
         pr = p.astype(jnp.bfloat16)
@@ -188,7 +193,7 @@
 
     for copy in sent_a:
         copy.wait_recv()
-    sent_b = sum_stage(1, part_b, x * y_n + y, stage_b, jnp.sum(part_a[...], axis=0))
+    sent_b = sum_stage(1, part_b, y * z_n + z, stage_b, jnp.sum(part_a[...], axis=0))
 
     for g in range(KV_HEADS):
         for n, out in enumerate((dk_ref, dv_ref)):
@@ -220,12 +225,13 @@
         copy.wait_send()
 
 
-def write_kernel(dq_ref, dk_ref, dv_ref, sg_ref, dq_out, dk_out, dv_out, sg_out, sem):
-    pairs = ((dq_ref, dq_out), (dk_ref, dk_out), (dv_ref, dv_out))
+def write_kernel(dq_ref, dk_ref, dv_ref, sg_ref, dq_out, dk_out, dv_out, sg_out, sg_row, sem):
+    sg_row[...] = sg_ref[0, :HEADS]
+    rows = [pl.ds(n * TOK // 4, TOK // 4) for n in range(4)]
+    pairs = [(dq_ref.at[0, r], dq_out.at[0, r]) for r in rows] + [(dk_ref, dk_out), (dv_ref, dv_out), (sg_row, sg_out)]
     copies = [pltpu.make_async_copy(src, dst, sem.at[n]) for n, (src, dst) in enumerate(pairs)]
     for copy in copies:
         copy.start()
-    sg_out[...] = sg_ref[0, :HEADS]
     for copy in copies:
         copy.wait()
 
@@ -249,20 +255,20 @@
             in_specs=[any_space] * 5,
             out_specs=(vmem_space,) * 4,
             scratch_shapes=[
-                pltpu.VMEM((HEADS, TOK, HEAD), bf16),
-                pltpu.VMEM((HEADS, TOK, HEAD), bf16),
-                pltpu.VMEM((KV_HEADS, 2 * TOK, HEAD), bf16),
-                pltpu.VMEM((KV_HEADS, 2 * TOK, HEAD), bf16),
+                pltpu.VMEM((KV_HEADS, TOK, GROUP * HEAD), bf16),
+                pltpu.VMEM((KV_HEADS, TOK, GROUP * HEAD), bf16),
+                pltpu.VMEM((2, TOK, KV_HEADS * HEAD), bf16),
+                pltpu.VMEM((2, KV_HEADS, TOK, HEAD), bf16),
                 pltpu.VMEM((2, KV_HEADS, TOK, HEAD), f32),
                 pltpu.VMEM((2, KV_HEADS, TOK, HEAD), bf16),
                 pltpu.VMEM((2, KV_HEADS, TOK, HEAD), bf16),
                 pltpu.VMEM((2 * TOK, TOK), f32),
                 pltpu.SMEM((HEADS,), f32),
                 pltpu.VMEM((HEADS, TOK), f32),
-                pltpu.VMEM((16, 1, HEAD), f32),
-                pltpu.VMEM((nd * nc // 16, 1, HEAD), f32),
-                pltpu.SemaphoreType.DMA((2, HEADS)),
-                pltpu.SemaphoreType.DMA((KV_HEADS, 2)),
+                pltpu.VMEM((nc // 2, 1, HEAD), f32),
+                pltpu.VMEM((nd * 2, 1, HEAD), f32),
+                pltpu.SemaphoreType.DMA((2, KV_HEADS)),
+                pltpu.SemaphoreType.DMA((2,)),
                 pltpu.SemaphoreType.DMA,
                 pltpu.SemaphoreType.DMA((KV_HEADS, 2)),
                 pltpu.SemaphoreType.DMA((KV_HEADS, 2)),
@@ -282,8 +288,8 @@
                 jax.ShapeDtypeStruct((HEADS,), f32),
             ),
             in_specs=[vmem_space] * 4,
-            out_specs=(any_space, any_space, any_space, vmem_space),
-            scratch_shapes=[pltpu.SemaphoreType.DMA((3,))],
+            out_specs=(any_space,) * 4,
+            scratch_shapes=[pltpu.VMEM((HEADS,), f32), pltpu.SemaphoreType.DMA((7,))],
             compiler_params=pltpu.CompilerParams(vmem_limit_bytes=1 << 20),
         )(*results)
 

time: 43.7 us -> 42.4 us (0.970)
  Pallas kernels: 43 us -> 41.6 us
    pallas_call x1, Pallas kernels: 41.6 us -> 40.7 us  [body(): pl.pallas_call(functools.partial(kernel, nd, nc, token_root), out_shape=(...]
    pallas_call x1, Pallas kernels: 1.41 us -> 0.94 us  [body(): pl.pallas_call(write_kernel, out_shape=(jax.ShapeDtypeStruct(queries.shap...]
where the time goes in v3:
time: 42.4 us; the launch traced here: 42.3 us
  Pallas kernels  41.6 us (98%)
  between operations  0.64 us (2%)
    pallas_call x1, Pallas kernels, body(): pl.pallas_call(functools.partial(kernel, nd, nc, token_root), out_shape=(...  40.7 us
    pallas_call x1, Pallas kernels, body(): pl.pallas_call(write_kernel, out_shape=(jax.ShapeDtypeStruct(queries.shap...  0.94 us

profile of v3, /device:TPU:1, one launch (start us, length us, event | category | flops | bytes accessed | tf_op | source)
XLA Modules:
  0.0 42.3 jit_solution(413622363960633976)
XLA Ops:
  0.6 40.7 %shard_map.84 = (bf16[1,128,2048]{2,1,0:T(8,128)(2,1)S(1)}, bf16[1,128,512]{2,1,0:T(8,128)(2,1)S(1)}, bf16[1,128,512]{2,1,0:T(8,128)(2,1)S(1)}, f32[1,128]{1,0:T(1,128)S(1)}) custom-call(bf16[1,128,2048]{2,1,0:T(8,128)(2,1)} %q_hbm.1, bf16[1,128,512]{2,1,0:T(8,128)(2,1)} %k_hbm.1, bf16[1,128,512]{2,1,0:T(8,128)(2,1)} %v_hbm.1, bf16[1,128,2048]{2,1,0:T(8,128)(2,1)} %do_hbm.1, ...), custom_call_target="tpu_custom_call" | custom-call | tf_op jit(solution)/shard_map/pallas_call | solution.py:247
  41.3 0.9 %shard_map.85 = (bf16[1,128,2048]{2,1,0:T(8,128)(2,1)}, bf16[1,128,512]{2,1,0:T(8,128)(2,1)}, bf16[1,128,512]{2,1,0:T(8,128)(2,1)}, f32[16]{0:T(128)}) custom-call(bf16[1,128,2048]{2,1,0:T(8,128)(2,1)S(1)} %get-tuple-element.8.dq_ref, bf16[1,128,512]{2,1,0:T(8,128)(2,1)S(1)} %get-tuple-element.9.dk_ref, bf16[1,128,512]{2,1,0:T(8,128)(2,1)S(1)} %get-tuple-element.10.dv_ref, ...), custom_call_target="tpu_custom_call" | custom-call | tf_op jit(solution)/shard_map/pallas_call | solution.py:282

commit v4 on v3

--- a/solution.py
+++ b/solution.py
@@ -41,7 +41,7 @@
     q_hbm, k_hbm, v_hbm, do_hbm, sinks_hbm,
     dq_ref, dk_ref, dv_ref, sg_ref,
     qv, dov, kv, prior, own, back, landed, bias, sinks_s, terms, part_a, part_b,
-    in_sem, kv_sem, sink_sem, halo_send, halo_recv, grad_send, grad_recv, sum_send, sum_recv,
+    in_sem, kv_sem, sink_sem, halo_send, halo_recv, grad_send, grad_recv, sum_send, sum_recv, round_sem,
 ):
     d = lax.axis_index("dp")
     c = lax.axis_index("ctx")
@@ -65,6 +65,12 @@
     stage_a.sort(key=far)
     stage_b.sort(key=far)
 
+    half = y_n // 2
+    near = [(0, 0, 1, 0), (0, 0, z_n - 1, 0), (0, 1, 0, 0), (0, y_n - 1, 0, 0)]
+    twice = [(0, 0, 2, 0), (0, 0, z_n - 2, 0), (0, 2, 0, 0), (0, y_n - 2, 0, 0)]
+    corner = [(0, dy, dz, 0) for dy in (2, y_n - 2) for dz in (2, z_n - 2)]
+    rounds = [near, near + twice, [(0, 0, z_n // 2, 0), (0, half, 0, 0)] + corner]
+
     barrier = pltpu.get_barrier_semaphore()
 
     def greet(device):
@@ -78,7 +84,7 @@
     def _():
         greet((d, right))
 
-    for offset in stage_a + stage_b:
+    for offset in stage_a + near:
         greet(at(*offset))
 
     sink_load = pltpu.make_async_copy(sinks_hbm, sinks_s, sink_sem)
@@ -94,7 +100,7 @@
         copy.start()
 
     as_int = lambda flag: jnp.where(flag, 1, 0)
-    pl.semaphore_wait(barrier, as_int(has_left) + as_int(has_right) + len(stage_a) + len(stage_b))
+    pl.semaphore_wait(barrier, as_int(has_left) + as_int(has_right) + len(stage_a) + len(near))
 
     halo = []
     for g in range(KV_HEADS):
@@ -128,6 +134,11 @@
             some = part.at[pl.ds(0, len(offsets))]
             return [remote(some, some, sum_send.at[n], sum_recv.at[n], at(*offsets[0]))]
         return []
+
+    for n, offsets in enumerate(rounds):
+        for offset in offsets:
+            pl.semaphore_signal(round_sem.at[n], inc=1, device_id=at(*offset), device_id_type=MESH)
+        pl.semaphore_wait(round_sem.at[n], len(offsets))
 
     grads = []
     for g in range(KV_HEADS):
@@ -276,6 +287,7 @@
                 pltpu.SemaphoreType.DMA((KV_HEADS, 2)),
                 pltpu.SemaphoreType.DMA((2,)),
                 pltpu.SemaphoreType.DMA((2,)),
+                pltpu.SemaphoreType.REGULAR((3,)),
             ],
             compiler_params=pltpu.CompilerParams(collective_id=0, has_side_effects=True),
         )(queries, keys, values, dout, sinks)

time: 42.4 us -> 39.9 us (0.941)
  Pallas kernels: 41.6 us -> 39.1 us
    pallas_call x1, Pallas kernels: 40.7 us -> 38.2 us  [body(): pl.pallas_call(functools.partial(kernel, nd, nc, token_root), out_shape=(...]
where the time goes in v4:
time: 39.9 us; the launch traced here: 39.8 us
  Pallas kernels  39.1 us (98%)
  between operations  0.64 us (2%)
    pallas_call x1, Pallas kernels, body(): pl.pallas_call(functools.partial(kernel, nd, nc, token_root), out_shape=(...  38.2 us
    pallas_call x1, Pallas kernels, body(): pl.pallas_call(write_kernel, out_shape=(jax.ShapeDtypeStruct(queries.shap...  0.94 us

profile of v4, /device:TPU:1, one launch (start us, length us, event | category | flops | bytes accessed | tf_op | source)
XLA Modules:
  0.0 39.8 jit_solution(115528420410408142)
XLA Ops:
  0.6 38.2 %shard_map.84 = (bf16[1,128,2048]{2,1,0:T(8,128)(2,1)S(1)}, bf16[1,128,512]{2,1,0:T(8,128)(2,1)S(1)}, bf16[1,128,512]{2,1,0:T(8,128)(2,1)S(1)}, f32[1,128]{1,0:T(1,128)S(1)}) custom-call(bf16[1,128,2048]{2,1,0:T(8,128)(2,1)} %q_hbm.1, bf16[1,128,512]{2,1,0:T(8,128)(2,1)} %k_hbm.1, bf16[1,128,512]{2,1,0:T(8,128)(2,1)} %v_hbm.1, bf16[1,128,2048]{2,1,0:T(8,128)(2,1)} %do_hbm.1, ...), custom_call_target="tpu_custom_call" | custom-call | tf_op jit(solution)/shard_map/pallas_call | solution.py:258
  38.8 0.9 %shard_map.85 = (bf16[1,128,2048]{2,1,0:T(8,128)(2,1)}, bf16[1,128,512]{2,1,0:T(8,128)(2,1)}, bf16[1,128,512]{2,1,0:T(8,128)(2,1)}, f32[16]{0:T(128)}) custom-call(bf16[1,128,2048]{2,1,0:T(8,128)(2,1)S(1)} %get-tuple-element.8.dq_ref, bf16[1,128,512]{2,1,0:T(8,128)(2,1)S(1)} %get-tuple-element.9.dk_ref, bf16[1,128,512]{2,1,0:T(8,128)(2,1)S(1)} %get-tuple-element.10.dv_ref, ...), custom_call_target="tpu_custom_call" | custom-call | tf_op jit(solution)/shard_map/pallas_call | solution.py:294
